TPU v7x, 32 devices: a whole 2x2x4 slice. The times are simulated.
32 devices in a mesh: pb: 8 (over z, core), ka: 4 (over y, x).
Axes of the slice: x: 2, y: 2, z: 4, core: 2. Of those that a mesh axis runs over, the one named last changes fastest.
Arguments:
- activations: bfloat16 [4, 1024, 768], P(None, ('pb', 'ka')), may hold values from -6 to 6
- attn_gain: float32 [768], replicated, may hold values from 0.1 to 1.9
- w_qkv: bfloat16 [768, 2304], replicated, may hold values from -0.21875 to 0.21875
- w_gate: bfloat16 [768, 768], replicated, may hold values from -0.21875 to 0.21875
- w_out: bfloat16 [768, 768], replicated, may hold values from -0.21875 to 0.21875
- pair_bias: bfloat16 [16, 1024, 1024], P(None, 'pb', 'ka'), may hold values from -240 to 240
- chain_ids: int32 [1024], replicated, may hold values from 0 to 5, as said below
- binder_flag: int32 [1024], replicated, may hold values from 0 to 1, as said below
- trans_gain: float32 [768], replicated, may hold values from 0.1 to 1.9
- w_up: bfloat16 [768, 3072], replicated, may hold values from -0.21875 to 0.21875
- w_down: bfloat16 [1536, 768], replicated, may hold values from -0.15625 to 0.15625
Outputs:
- updated: bfloat16 [4, 1024, 768], P(None, ('pb', 'ka'))
Inputs may be any that keep to these rules, and one draw needn't show every extreme that they name: `chain_ids`: chain ids never fall along the tokens; every chain has at least one token. `binder_flag`: all tokens of one chain carry the same flag.
All inputs are finite; a program needn't handle non-finite values.
Results may differ from a plain program's by a relative error of at most 0.0056.
Values may be sent and summed in bfloat16 or wider, within the bound.
No kernel may reach another device: no remote copies, remote signals or barrier semaphores. Data moves between devices by JAX's collectives and lax.ppermute only.
A program may use at most 128 MiB of HBM per device.

v0:
```python
import math
import jax
import jax.numpy as jnp
from jax import lax
from jax.sharding import PartitionSpec as P

epsilon = 1e-05
masked_score = -1000000000.0


def spread_2(value, axis, source):
    kept = jnp.where(lax.axis_index(axis) == source, value, 0).astype(value.dtype)
    return lax.psum(kept, axis)


def joined(value, axis, join):
    pieces = jax.tree.map(lambda part: lax.all_gather(part, axis), value)
    head = jax.tree.map(lambda part: part[0], pieces)
    tail = jax.tree.map(lambda part: part[1:], pieces)
    total, _ = lax.scan(lambda total, share: (join(total, share), None), head, tail)
    return total


def layer_norm(values, scales):
    centred = values - jnp.mean(values, axis=-1, keepdims=True)
    spread = jnp.mean(centred * centred, axis=-1, keepdims=True)
    return centred * lax.rsqrt(spread + epsilon) * scales


def block_stats(query_rows, key_block, value_block, bias_tile, allowed):
    head_count = bias_tile.shape[0]
    query_heads = query_rows.reshape(query_rows.shape[0], head_count, -1)
    key_heads = key_block.reshape(key_block.shape[0], head_count, -1)
    value_heads = value_block.reshape(value_block.shape[0], head_count, -1)
    head_size = query_heads.shape[-1]
    scores = jnp.einsum(
        "qhd,khd->hqk", query_heads, key_heads, preferred_element_type=jnp.float32
    ) / math.sqrt(head_size)
    scores = scores + bias_tile.astype(jnp.float32)
    best_score = jnp.max(jnp.where(allowed[None], scores, masked_score), axis=-1)
    weights = jnp.where(allowed[None], jnp.exp(scores - best_score[..., None]), 0.0)
    row_sum = jnp.sum(weights, axis=-1)
    block_out = jnp.einsum(
        "hqk,khd->qhd",
        weights.astype(jnp.bfloat16),
        value_heads,
        preferred_element_type=jnp.float32,
    )
    return (best_score.T, row_sum.T, block_out.reshape(query_rows.shape[0], -1))


def merge_pair(earlier, later):
    earlier_top, earlier_sum, earlier_out = earlier
    later_top, later_sum, later_out = later
    overall = jnp.maximum(earlier_top, later_top)
    earlier_factor = jnp.exp(earlier_top - overall)
    later_factor = jnp.exp(later_top - overall)
    row_sum = earlier_factor * earlier_sum + later_factor * later_sum
    shaped = earlier_out.shape[:-1] + (overall.shape[-1], -1)
    merged_out = earlier_factor[..., None] * earlier_out.reshape(shaped) + later_factor[
        ..., None
    ] * later_out.reshape(shaped)
    return (overall, row_sum, merged_out.reshape(earlier_out.shape))


def body(
    activations,
    attn_gain,
    w_qkv,
    w_gate,
    w_out,
    pair_bias,
    chain_ids,
    binder_flag,
    trans_gain,
    w_up,
    w_down,
):
    samples, own_rows, model_width = activations.shape
    head_count, query_count, key_count = pair_bias.shape
    pb_ratio = lax.axis_size("pb") // lax.axis_size("ka")
    normed = layer_norm(activations.astype(jnp.float32), attn_gain).astype(jnp.bfloat16)
    flat_normed = normed.reshape(-1, model_width)
    gate_pre = jnp.dot(flat_normed, w_gate, preferred_element_type=jnp.float32).reshape(
        samples, own_rows, model_width
    )
    queries = jnp.dot(flat_normed, w_qkv[:, :model_width], preferred_element_type=jnp.float32)
    queries = queries.astype(jnp.bfloat16).reshape(samples, own_rows, model_width)
    queries, block_normed = (
        lax.all_gather(queries, "ka", axis=1, tiled=True),
        lax.all_gather(normed, "ka", axis=1, tiled=True),
    )
    input_parts = []
    for within in range(pb_ratio):
        source_index = lax.axis_index("ka") * pb_ratio + within
        input_parts.append(spread_2(block_normed, "pb", source_index))
    key_inputs = jnp.concatenate(input_parts, axis=1).reshape(-1, model_width)
    key_value = jnp.dot(key_inputs, w_qkv[:, model_width:], preferred_element_type=jnp.float32)
    key_block = (
        key_value[:, :model_width].astype(jnp.bfloat16).reshape(samples, key_count, model_width)
    )
    value_block = (
        key_value[:, model_width:].astype(jnp.bfloat16).reshape(samples, key_count, model_width)
    )
    query_start = lax.axis_index("pb") * query_count
    key_start = lax.axis_index("ka") * key_count
    row_chain = lax.dynamic_slice_in_dim(chain_ids, query_start, query_count, 0)
    row_binder = lax.dynamic_slice_in_dim(binder_flag, query_start, query_count, 0)
    col_chain = lax.dynamic_slice_in_dim(chain_ids, key_start, key_count, 0)
    col_binder = lax.dynamic_slice_in_dim(binder_flag, key_start, key_count, 0)
    allowed = (
        (row_binder[:, None] > 0)
        | (col_binder[None, :] > 0)
        | (row_chain[:, None] == col_chain[None, :])
    )

    def per_sample(operands):
        return block_stats(operands[0], operands[1], operands[2], pair_bias, allowed)

    block_tops, block_sums, block_outs = lax.map(per_sample, (queries, key_block, value_block))
    block_tops, block_sums, block_outs = joined(
        (block_tops, block_sums, block_outs), "ka", merge_pair
    )
    offset = lax.axis_index("ka") * own_rows
    row_sum = lax.dynamic_slice_in_dim(block_sums, offset, own_rows, 1)
    row_out = lax.dynamic_slice_in_dim(block_outs, offset, own_rows, 1)
    attention = (row_out.reshape(samples, own_rows, head_count, -1) / row_sum[..., None]).reshape(
        samples, own_rows, model_width
    )
    gated = (jax.nn.sigmoid(gate_pre) * attention).astype(jnp.bfloat16)
    mixed = activations.astype(jnp.float32) + jnp.dot(
        gated.reshape(-1, model_width), w_out, preferred_element_type=jnp.float32
    ).reshape(samples, own_rows, model_width)
    trans_normed = layer_norm(mixed, trans_gain).astype(jnp.bfloat16)
    both_parts = jnp.dot(
        trans_normed.reshape(-1, model_width), w_up, preferred_element_type=jnp.float32
    )
    hidden_width = w_down.shape[0]
    hidden = (jax.nn.silu(both_parts[:, :hidden_width]) * both_parts[:, hidden_width:]).astype(
        jnp.bfloat16
    )
    updated = mixed + jnp.dot(hidden, w_down, preferred_element_type=jnp.float32).reshape(
        samples, own_rows, model_width
    )
    return updated.astype(jnp.bfloat16)


def solution(mesh):
    placed = (
        P(None, ("pb", "ka"), None),
        P(),
        P(),
        P(),
        P(),
        P(None, "pb", "ka"),
        P(),
        P(),
        P(),
        P(),
        P(),
    )
    return jax.shard_map(
        body, mesh=mesh, in_specs=placed, out_specs=P(None, ("pb", "ka"), None), check_vma=False
    )
```

profile of v0, /device:TPU:0, one launch (start us, length us, event | category | flops | bytes accessed | tf_op | source)
XLA Modules:
  0.0 271.9 jit_solution(7800680378099622818)
XLA Ops:
  6.5 1.2 convert_reduce_fusion
  7.7 1.1 fusion.33
  8.9 1.1 fusion.35
  10.0 12.7 %all_gather.25 = bf16[4,128,768]{2,1,0:T(8,128)(2,1)S(1)} all-gather(bf16[4,32,768]{2,1,0:T(8,128)(2,1)S(1)} %fusion.35), channel_id=1, replica_groups=mesh['pb'=8,'ka'=4] {'ka'}, dimensions={1}, use_global_device_ids=true | all-gather | bytes 983040 | tf_op jit(solution)/shard_map/all_gather | solution.py:91
  22.7 1.3 broadcast_select_fusion.1
  25.6 1.6 fusion.25
  27.3 12.1 %all_gather.24 = bf16[4,128,768]{2,0,1:T(4,128)(2,1)S(1)} all-gather(bf16[4,32,768]{2,0,1:T(4,128)(2,1)S(1)} %copy.24), channel_id=1, replica_groups=mesh['pb'=8,'ka'=4] {'ka'}, dimensions={1}, use_global_device_ids=true | all-gather | bytes 983040 | tf_op jit(solution)/shard_map/all_gather | solution.py:90
  39.5 1.3 copy.25
  42.3 44.2 %all-reduce.3.cloned.1.call-done = (bf16[4,128,768]{2,1,0:T(8,128)(2,1)}, bf16[4,128,768]{2,1,0:T(8,128)(2,1)}) async-done(((bf16[4,128,768]{2,1,0:T(8,128)(2,1)}, bf16[4,128,768]{2,1,0:T(8,128)(2,1)}), (bf16[4,128,768]{2,1,0:T(8,128)(2,1)}, bf16[4,128,768]{2,1,0:T(8,128)(2,1)})) %all-reduce.3.cloned.1.call-update) | async-done | bytes 1572880 | tf_op jit(solution)/shard_map/psum | solution.py:13
  86.5 1.5 pad_maximum_fusion
  88.0 4.5 %convolution_convert_fusion = bf16[1024,1536]{1,0:T(8,128)(2,1)S(1)} fusion(bf16[1024,768]{1,0:T(8,128)(2,1)S(1)} %bitcast.100, bf16[768,2304]{1,0:T(8,128)(2,1)} %param.17), kind=kOutput, calls=%fused_computation.28 | convolution fusion | flops 2417491968 | bytes 7077888 | tf_op jit(solution)/shard_map/dot_general | solution.py:98
  92.5 1.9 fusion.48
  94.4 50.9 %while.30 = (s32[]{:T(128)}, f32[4,128,16]{1,2,0:T(8,128)}, f32[4,128,16]{1,2,0:T(8,128)}, f32[4,128,768]{2,1,0:T(8,128)}, bf16[4,128,768]{1,2,0:T(8,128)(2,1)},...) while((s32[]{:T(128)}, f32[4,128,16]{1,2,0:T(8,128)}, ...), condition=%wide.region_7.8_spmd.clone, body=%wide.region_4.7_spmd.clone.sunk | while | flops 106524672 | bytes 14295217 | solution.py:120
  96.7 3.2 %select_reduce_fusion.2 = (f32[16,128]{1,0:T(8,128)S(1)}, f32[16,128,256]{2,1,0:T(8,128)}) fusion(pred[128,256]{1,0:T(8,128)(4,1)S(1)} %compare_or_fusion.2, bf16[16,128,256]{2,1,0:T(8,128)(2,1)} %get-tuple-element.395, bf16[128,16,48]{0,2,1:T(8,128)(2,1)S(1)} %bitcast.97, bf16[256,16,48]{0,2,1:T(8,128)(2,1)S(1)} %bitcast.93), kind=kOutput, calls=%fused_computation.12.clone.1 | convolution fusion | flops 52951040 | bytes 3776512 | tf_op jit(solution)/shard_map/while/body/eval_jaxpr/qhd,khd->hqk/dot_general | solution.py:36
  99.8 1.0 constant_dynamic-slice_fusion.12
  101.1 2.2 fusion.78
  104.2 2.3 fusion.77
  107.1 1.0 constant_dynamic-slice_fusion.11
  109.4 3.2 %select_reduce_fusion.2 = (f32[16,128]{1,0:T(8,128)S(1)}, f32[16,128,256]{2,1,0:T(8,128)}) fusion(pred[128,256]{1,0:T(8,128)(4,1)S(1)} %compare_or_fusion.2, bf16[16,128,256]{2,1,0:T(8,128)(2,1)} %get-tuple-element.395, bf16[128,16,48]{0,2,1:T(8,128)(2,1)S(1)} %bitcast.97, bf16[256,16,48]{0,2,1:T(8,128)(2,1)S(1)} %bitcast.93), kind=kOutput, calls=%fused_computation.12.clone.1 | convolution fusion | flops 52951040 | bytes 3776512 | tf_op jit(solution)/shard_map/while/body/eval_jaxpr/qhd,khd->hqk/dot_general | solution.py:36
  112.6 1.0 constant_dynamic-slice_fusion.12
  113.8 2.2 fusion.78
  116.9 2.3 fusion.77
  122.1 3.2 %select_reduce_fusion.2 = (f32[16,128]{1,0:T(8,128)S(1)}, f32[16,128,256]{2,1,0:T(8,128)}) fusion(pred[128,256]{1,0:T(8,128)(4,1)S(1)} %compare_or_fusion.2, bf16[16,128,256]{2,1,0:T(8,128)(2,1)} %get-tuple-element.395, bf16[128,16,48]{0,2,1:T(8,128)(2,1)S(1)} %bitcast.97, bf16[256,16,48]{0,2,1:T(8,128)(2,1)S(1)} %bitcast.93), kind=kOutput, calls=%fused_computation.12.clone.1 | convolution fusion | flops 52951040 | bytes 3776512 | tf_op jit(solution)/shard_map/while/body/eval_jaxpr/qhd,khd->hqk/dot_general | solution.py:36
  126.5 2.2 fusion.78
  129.7 2.3 fusion.77
  134.8 3.2 %select_reduce_fusion.2 = (f32[16,128]{1,0:T(8,128)S(1)}, f32[16,128,256]{2,1,0:T(8,128)}) fusion(pred[128,256]{1,0:T(8,128)(4,1)S(1)} %compare_or_fusion.2, bf16[16,128,256]{2,1,0:T(8,128)(2,1)} %get-tuple-element.395, bf16[128,16,48]{0,2,1:T(8,128)(2,1)S(1)} %bitcast.97, bf16[256,16,48]{0,2,1:T(8,128)(2,1)S(1)} %bitcast.93), kind=kOutput, calls=%fused_computation.12.clone.1 | convolution fusion | flops 52951040 | bytes 3776512 | tf_op jit(solution)/shard_map/while/body/eval_jaxpr/qhd,khd->hqk/dot_general | solution.py:36
  139.2 2.2 fusion.78
  142.4 2.3 fusion.77
  146.0 8.5 %all-gather = f32[16,128,16]{1,2,0:T(8,128)S(1)} all-gather(f32[4,128,16]{1,2,0:T(8,128)S(1)} %copy-done.3), channel_id=2, replica_groups=mesh['pb'=8,'ka'=4] {'ka'}, dimensions={0}, use_global_device_ids=true | all-gather | bytes 163840 | tf_op jit(solution)/shard_map/all_gather | solution.py:17
  154.5 9.6 %all-gather.1 = f32[16,128,16]{1,2,0:T(8,128)S(1)} all-gather(f32[4,128,16]{1,2,0:T(8,128)S(1)} %copy-done.4), channel_id=3, replica_groups=mesh['pb'=8,'ka'=4] {'ka'}, dimensions={0}, use_global_device_ids=true | all-gather | bytes 163840 | tf_op jit(solution)/shard_map/all_gather | solution.py:17
  164.2 51.0 %all-gather.5.cloned.1.call-done = f32[16,128,768]{2,1,0:T(8,128)} async-done(((f32[4,128,768]{2,1,0:T(8,128)}), f32[16,128,768]{2,1,0:T(8,128)}) %all-gather.5.cloned.1.call-update) | async-done | bytes 6291472 | tf_op jit(solution)/shard_map/all_gather | solution.py:17
  215.2 2.7 slice.60
  217.9 3.0 %copy.29 = f32[4,128,768]{1,2,0:T(8,128)} copy(f32[4,128,768]{2,1,0:T(8,128)} %slice.60) | data formatting | bytes 3145728 | tf_op jit(solution)/shard_map/while | solution.py:20
  220.9 4.9 %slice.63 = f32[12,128,768]{2,1,0:T(8,128)} slice(f32[16,128,768]{2,1,0:T(8,128)} %all-gather.5.cloned.1.call-done), slice={[4:16], [0:128], [0:768]} | slice | bytes 9437184 | tf_op jit(solution)/shard_map/slice | solution.py:19
  225.8 27.0 %while.29 = (s32[]{:T(128)}, f32[4,128,16]{1,2,0:T(8,128)S(1)}, f32[4,128,16]{1,2,0:T(8,128)S(1)}, f32[4,128,768]{1,2,0:T(8,128)}, f32[3,4,128,16]{2,3,1,0:T(8,1...) while((s32[]{:T(128)}, f32[4,128,16]{1,2,0:T(8,128)S(1)}, ...), condition=%wide.region_9.10_spmd, body=%wide.region_8.9_spmd.sunk | while | flops 1228802 | bytes 11337821 | solution.py:20
  225.8 2.7 constant_dynamic-slice_fusion.9
  228.6 3.0 %copy.46 = f32[1,4,128,768]{2,3,1,0:T(8,128)} copy(f32[1,4,128,768]{3,2,1,0:T(8,128)} %constant_dynamic-slice_fusion.9) | data formatting | bytes 3145728 | tf_op jit(solution)/shard_map/while/body/jit(dynamic_index_in_dim)/dynamic_slice | solution.py:20
  231.6 3.2 %fusion.72 = f32[4,128,768]{1,2,0:T(8,128)} fusion(f32[1,4,128,768]{2,3,1,0:T(8,128)} %copy.46, f32[4,128,768]{1,2,0:T(8,128)} %get-tuple-element.413, f32[4,128,16]{1,2,0:T(8,128)S(1)} %get-tuple-element.345, f32[4,128,16]{1,2,0:T(8,128)S(1)} %get-tuple-element.346), kind=kLoop, calls=%fused_computation.2.clone.1 | loop fusion | flops 1179648 | bytes 4784128 | tf_op jit(solution)/shard_map/while/body/eval_jaxpr/add | solution.py:60
  234.8 2.7 constant_dynamic-slice_fusion.9
  237.6 3.0 %copy.46 = f32[1,4,128,768]{2,3,1,0:T(8,128)} copy(f32[1,4,128,768]{3,2,1,0:T(8,128)} %constant_dynamic-slice_fusion.9) | data formatting | bytes 3145728 | tf_op jit(solution)/shard_map/while/body/jit(dynamic_index_in_dim)/dynamic_slice | solution.py:20
  240.6 3.2 %fusion.72 = f32[4,128,768]{1,2,0:T(8,128)} fusion(f32[1,4,128,768]{2,3,1,0:T(8,128)} %copy.46, f32[4,128,768]{1,2,0:T(8,128)} %get-tuple-element.413, f32[4,128,16]{1,2,0:T(8,128)S(1)} %get-tuple-element.345, f32[4,128,16]{1,2,0:T(8,128)S(1)} %get-tuple-element.346), kind=kLoop, calls=%fused_computation.2.clone.1 | loop fusion | flops 1179648 | bytes 4784128 | tf_op jit(solution)/shard_map/while/body/eval_jaxpr/add | solution.py:60
  243.8 2.7 constant_dynamic-slice_fusion.9
  246.6 3.0 %copy.46 = f32[1,4,128,768]{2,3,1,0:T(8,128)} copy(f32[1,4,128,768]{3,2,1,0:T(8,128)} %constant_dynamic-slice_fusion.9) | data formatting | bytes 3145728 | tf_op jit(solution)/shard_map/while/body/jit(dynamic_index_in_dim)/dynamic_slice | solution.py:20
  249.6 3.2 %fusion.72 = f32[4,128,768]{1,2,0:T(8,128)} fusion(f32[1,4,128,768]{2,3,1,0:T(8,128)} %copy.46, f32[4,128,768]{1,2,0:T(8,128)} %get-tuple-element.413, f32[4,128,16]{1,2,0:T(8,128)S(1)} %get-tuple-element.345, f32[4,128,16]{1,2,0:T(8,128)S(1)} %get-tuple-element.346), kind=kLoop, calls=%fused_computation.2.clone.1 | loop fusion | flops 1179648 | bytes 4784128 | tf_op jit(solution)/shard_map/while/body/eval_jaxpr/add | solution.py:60
  252.8 3.0 %copy.31 = f32[4,128,768]{2,1,0:T(8,128)} copy(f32[4,128,768]{1,2,0:T(8,128)} %get-tuple-element.95) | data formatting | bytes 3145728 | tf_op jit(solution)/shard_map/while | solution.py:20
  256.4 1.2 div.37
  257.5 2.7 fusion.49
  260.6 3.2 %fusion.54 = f32[128,3072]{1,0:T(8,128)S(1)} fusion(bf16[128,768]{1,0:T(8,128)(2,1)S(1)} %bitcast.101, bf16[768,3072]{1,0:T(8,128)(2,1)} %param.24), kind=kOutput, calls=%fused_computation.74 | convolution fusion | flops 603979776 | bytes 6488064 | tf_op jit(solution)/shard_map/dot_general | solution.py:135
  (129 shorter events, 23.3 us)
Async XLA Ops:
  6.5 257.2 %copy-start = (bf16[1536,768]{1,0:T(8,128)(2,1)S(1)}, bf16[1536,768]{1,0:T(8,128)(2,1)}, u32[]{:S(2)}) copy-start(bf16[1536,768]{1,0:T(8,128)(2,1)} %param.25) | copy-start | bytes 7077892
  6.5 80.0 %all-reduce.3.cloned.1.call-start = ((), (), s32[]{:S(2)}) async-start(), calls=%async_computation.1 | async-start | bytes 3145728 | tf_op jit(solution)/shard_map/psum | solution.py:13
  7.7 1.2 copy-start.5
  8.9 1.1 copy-start.11
  24.0 191.2 %all-gather.5.cloned.1.call-start = ((), (), s32[]{:S(2)}) async-start(), calls=%async_computation | async-start | bytes 7864320 | tf_op jit(solution)/shard_map/all_gather | solution.py:17
  94.4 5.5 %copy-start.7 = (s32[128]{0:T(128)}, s32[128]{0:T(128)S(1)}, u32[]{:S(2)}) copy-start(s32[128]{0:T(128)S(1)} %get-tuple-element.400) | copy-start | bytes 1540 | tf_op jit(solution)/shard_map/while
  94.4 5.5 %copy-start.9 = (pred[128]{0:T(512)(128)(4,1)}, pred[128]{0:T(512)(128)(4,1)S(1)}, u32[]{:S(2)}) copy-start(pred[128]{0:T(512)(128)(4,1)S(1)} %get-tuple-element.398) | copy-start | bytes 388 | tf_op jit(solution)/shard_map/while
  96.6 3.2 %copy-start.1 = (pred[128,256]{1,0:T(8,128)(4,1)}, pred[128,256]{1,0:T(8,128)(4,1)S(1)}, u32[]{:S(2)}) copy-start(pred[128,256]{1,0:T(8,128)(4,1)S(1)} %compare_or_fusion.2) | copy-start | bytes 98308 | tf_op jit(solution)/shard_map/while
  103.2 1.0 copy-start.2
  103.4 3.7 %copy-start.8 = (s32[128]{0:T(128)S(1)}, s32[128]{0:T(128)}, u32[]{:S(2)}) copy-start(s32[128]{0:T(128)} %copy-done.7) | copy-start | bytes 1540 | tf_op jit(solution)/shard_map/while
  103.4 3.7 %copy-start.10 = (pred[128]{0:T(512)(128)(4,1)S(1)}, pred[128]{0:T(512)(128)(4,1)}, u32[]{:S(2)}) copy-start(pred[128]{0:T(512)(128)(4,1)} %copy-done.9) | copy-start | bytes 388 | tf_op jit(solution)/shard_map/while
  107.1 5.5 %copy-start.7 = (s32[128]{0:T(128)}, s32[128]{0:T(128)S(1)}, u32[]{:S(2)}) copy-start(s32[128]{0:T(128)S(1)} %get-tuple-element.400) | copy-start | bytes 1540 | tf_op jit(solution)/shard_map/while
  107.1 5.5 %copy-start.9 = (pred[128]{0:T(512)(128)(4,1)}, pred[128]{0:T(512)(128)(4,1)S(1)}, u32[]{:S(2)}) copy-start(pred[128]{0:T(512)(128)(4,1)S(1)} %get-tuple-element.398) | copy-start | bytes 388 | tf_op jit(solution)/shard_map/while
  109.4 3.2 %copy-start.1 = (pred[128,256]{1,0:T(8,128)(4,1)}, pred[128,256]{1,0:T(8,128)(4,1)S(1)}, u32[]{:S(2)}) copy-start(pred[128,256]{1,0:T(8,128)(4,1)S(1)} %compare_or_fusion.2) | copy-start | bytes 98308 | tf_op jit(solution)/shard_map/while
  116.0 1.0 copy-start.2
  116.1 3.7 %copy-start.8 = (s32[128]{0:T(128)S(1)}, s32[128]{0:T(128)}, u32[]{:S(2)}) copy-start(s32[128]{0:T(128)} %copy-done.7) | copy-start | bytes 1540 | tf_op jit(solution)/shard_map/while
  116.1 3.7 %copy-start.10 = (pred[128]{0:T(512)(128)(4,1)S(1)}, pred[128]{0:T(512)(128)(4,1)}, u32[]{:S(2)}) copy-start(pred[128]{0:T(512)(128)(4,1)} %copy-done.9) | copy-start | bytes 388 | tf_op jit(solution)/shard_map/while
  119.8 5.5 %copy-start.7 = (s32[128]{0:T(128)}, s32[128]{0:T(128)S(1)}, u32[]{:S(2)}) copy-start(s32[128]{0:T(128)S(1)} %get-tuple-element.400) | copy-start | bytes 1540 | tf_op jit(solution)/shard_map/while
  119.8 5.5 %copy-start.9 = (pred[128]{0:T(512)(128)(4,1)}, pred[128]{0:T(512)(128)(4,1)S(1)}, u32[]{:S(2)}) copy-start(pred[128]{0:T(512)(128)(4,1)S(1)} %get-tuple-element.398) | copy-start | bytes 388 | tf_op jit(solution)/shard_map/while
  122.1 3.2 %copy-start.1 = (pred[128,256]{1,0:T(8,128)(4,1)}, pred[128,256]{1,0:T(8,128)(4,1)S(1)}, u32[]{:S(2)}) copy-start(pred[128,256]{1,0:T(8,128)(4,1)S(1)} %compare_or_fusion.2) | copy-start | bytes 98308 | tf_op jit(solution)/shard_map/while
  128.7 1.0 copy-start.2
  128.9 3.7 %copy-start.8 = (s32[128]{0:T(128)S(1)}, s32[128]{0:T(128)}, u32[]{:S(2)}) copy-start(s32[128]{0:T(128)} %copy-done.7) | copy-start | bytes 1540 | tf_op jit(solution)/shard_map/while
  128.9 3.7 %copy-start.10 = (pred[128]{0:T(512)(128)(4,1)S(1)}, pred[128]{0:T(512)(128)(4,1)}, u32[]{:S(2)}) copy-start(pred[128]{0:T(512)(128)(4,1)} %copy-done.9) | copy-start | bytes 388 | tf_op jit(solution)/shard_map/while
  132.5 5.5 %copy-start.7 = (s32[128]{0:T(128)}, s32[128]{0:T(128)S(1)}, u32[]{:S(2)}) copy-start(s32[128]{0:T(128)S(1)} %get-tuple-element.400) | copy-start | bytes 1540 | tf_op jit(solution)/shard_map/while
  132.5 5.5 %copy-start.9 = (pred[128]{0:T(512)(128)(4,1)}, pred[128]{0:T(512)(128)(4,1)S(1)}, u32[]{:S(2)}) copy-start(pred[128]{0:T(512)(128)(4,1)S(1)} %get-tuple-element.398) | copy-start | bytes 388 | tf_op jit(solution)/shard_map/while
  134.8 3.2 %copy-start.1 = (pred[128,256]{1,0:T(8,128)(4,1)}, pred[128,256]{1,0:T(8,128)(4,1)S(1)}, u32[]{:S(2)}) copy-start(pred[128,256]{1,0:T(8,128)(4,1)S(1)} %compare_or_fusion.2) | copy-start | bytes 98308 | tf_op jit(solution)/shard_map/while
  141.4 1.0 copy-start.2
  141.6 3.7 %copy-start.8 = (s32[128]{0:T(128)S(1)}, s32[128]{0:T(128)}, u32[]{:S(2)}) copy-start(s32[128]{0:T(128)} %copy-done.7) | copy-start | bytes 1540 | tf_op jit(solution)/shard_map/while
  141.6 3.7 %copy-start.10 = (pred[128]{0:T(512)(128)(4,1)S(1)}, pred[128]{0:T(512)(128)(4,1)}, u32[]{:S(2)}) copy-start(pred[128]{0:T(512)(128)(4,1)} %copy-done.9) | copy-start | bytes 388 | tf_op jit(solution)/shard_map/while
  145.3 0.8 copy-start.3
  145.3 9.2 %copy-start.4 = (f32[4,128,16]{1,2,0:T(8,128)S(1)}, f32[4,128,16]{1,2,0:T(8,128)}, u32[]{:S(2)}) copy-start(f32[4,128,16]{1,2,0:T(8,128)} %get-tuple-element.93) | copy-start | bytes 98308
  255.8 1.7 copy-start.6
  255.8 1.7 copy-start.12
  255.8 1.7 copy-start.13
  257.5 2.9 %copy-start.14 = (f32[768]{0:T(1024)S(1)}, f32[768]{0:T(1024)}, u32[]{:S(2)}) copy-start(f32[768]{0:T(1024)} %param.23) | copy-start | bytes 9220
Sparse Core Ops, SparseCore 0:
  24.1 62.3 all-reduce.2
  145.4 69.6 all-gather.4
where the time goes:
time: 274 us; the launch traced here: 272 us
  waiting for transfers between devices  95.2 us (35%)
  local copies, waits for them, and re-layouts  58 us (21%)
  blocking collectives  42.9 us (16%)
  matrix products  33.9 us (12%)
  other arithmetic  27.9 us (10%)
  between operations  13.6 us (5%)
    all_gather x1, waiting for transfers between devices, joined(): pieces = jax.tree.map(lambda part: lax.all_gather(part, axis), value)  51 us
    psum x1, waiting for transfers between devices, spread_2(): return lax.psum(kept, axis)  44.2 us
    all_gather x2, blocking collectives, joined(): pieces = jax.tree.map(lambda part: lax.all_gather(part, axis), value)  18.1 us
    dynamic_slice x6, local copies, waits for them, and re-layouts, joined(): lax.scan(lambda total, share: (join(total, share), None), head, tail)  17.2 us
    dynamic_slice x20, local copies, waits for them, and re-layouts, body(): lax.map(per_sample, (queries, key_block, value_block))  13.4 us
    dot_general x4, matrix products, block_stats(): jnp.einsum('qhd,khd->hqk', query_heads, key_heads, preferred_element_type...  12.7 us
    all_gather x1, blocking collectives, body(): lax.all_gather(normed, 'ka', axis=1, tiled=True)  12.7 us
    all_gather x1, blocking collectives, body(): lax.all_gather(queries, 'ka', axis=1, tiled=True)  12.1 us
  transfers between devices with their start and end apart: 2, of which 2 were waited for; matrix products, arithmetic and copies ran while one was open for 2% of the time, Pallas kernels for 0%

commit v1 on v0

--- a/solution.py
+++ b/solution.py
@@ -8,9 +8,15 @@
 masked_score = -1000000000.0
 
 
+def summed_here(x, axis):
+    parts = lax.all_gather(x, axis, axis=0, tiled=False)
+    total = parts.sum(axis=0)
+    return total
+
+
 def spread_2(value, axis, source):
     kept = jnp.where(lax.axis_index(axis) == source, value, 0).astype(value.dtype)
-    return lax.psum(kept, axis)
+    return summed_here(kept, axis)
 
 
 def joined(value, axis, join):

time: 274 us -> 345 us (1.26)
  waiting for transfers between devices: 95.2 us -> 158 us
  other arithmetic: 27.9 us -> 36.2 us
    all_gather x0 -> x2, waiting for transfers between devices: none -> 107 us  [summed_here(): parts = lax.all_gather(x, axis, axis=0, tiled=False)]
    psum x1 -> x0, waiting for transfers between devices: 44.2 us -> none  [spread_2(): return lax.psum(kept, axis)]
    reduce_sum x0 -> x2, other arithmetic: none -> 8.54 us  [summed_here(): total = parts.sum(axis=0)]
  transfers between devices with their start and end apart: 2 -> 3, of which waited for: 2 -> 3; matrix products, arithmetic and copies ran while one was open for 2% -> 3% of each run, Pallas kernels for 0% -> 0%
where the time goes in v1:
time: 345 us; the launch traced here: 344 us
  waiting for transfers between devices  158 us (46%)
  local copies, waits for them, and re-layouts  57.9 us (17%)
  blocking collectives  43.8 us (13%)
  other arithmetic  36.2 us (10%)
  matrix products  34 us (10%)
  between operations  13.3 us (4%)
    all_gather x2, waiting for transfers between devices, summed_here(): parts = lax.all_gather(x, axis, axis=0, tiled=False)  107 us
    all_gather x1, waiting for transfers between devices, joined(): pieces = jax.tree.map(lambda part: lax.all_gather(part, axis), value)  50 us
    all_gather x2, blocking collectives, joined(): pieces = jax.tree.map(lambda part: lax.all_gather(part, axis), value)  19 us
    dynamic_slice x6, local copies, waits for them, and re-layouts, joined(): lax.scan(lambda total, share: (join(total, share), None), head, tail)  17.2 us
    dynamic_slice x20, local copies, waits for them, and re-layouts, body(): lax.map(per_sample, (queries, key_block, value_block))  13.4 us
    dot_general x4, matrix products, block_stats(): jnp.einsum('qhd,khd->hqk', query_heads, key_heads, preferred_element_type...  12.8 us
    all_gather x1, blocking collectives, body(): lax.all_gather(normed, 'ka', axis=1, tiled=True)  12.7 us
    all_gather x1, blocking collectives, body(): lax.all_gather(queries, 'ka', axis=1, tiled=True)  12.1 us
  transfers between devices with their start and end apart: 3, of which 3 were waited for; matrix products, arithmetic and copies ran while one was open for 3% of the time, Pallas kernels for 0%

profile of v1, /device:TPU:0, one launch (start us, length us, event | category | flops | bytes accessed | tf_op | source)
XLA Modules:
  0.0 343.6 jit_solution(12538556577782780943)
XLA Ops:
  6.5 1.2 convert_reduce_fusion
  7.7 1.1 fusion.33
  8.9 1.1 fusion.35
  10.0 12.7 %all_gather.37 = bf16[4,128,768]{2,1,0:T(8,128)(2,1)S(1)} all-gather(bf16[4,32,768]{2,1,0:T(8,128)(2,1)S(1)} %fusion.35), channel_id=1, replica_groups=mesh['pb'=8,'ka'=4] {'ka'}, dimensions={1}, use_global_device_ids=true | all-gather | bytes 983040 | tf_op jit(solution)/shard_map/all_gather | solution.py:97
  22.7 1.3 broadcast_select_fusion.1
  26.3 1.6 fusion.25
  28.1 12.1 %all_gather.36 = bf16[4,128,768]{2,0,1:T(4,128)(2,1)S(1)} all-gather(bf16[4,32,768]{2,0,1:T(4,128)(2,1)S(1)} %copy.24), channel_id=1, replica_groups=mesh['pb'=8,'ka'=4] {'ka'}, dimensions={1}, use_global_device_ids=true | all-gather | bytes 983040 | tf_op jit(solution)/shard_map/all_gather | solution.py:96
  40.2 1.3 copy.25
  43.0 46.1 %all-gather.9.cloned.1.call-done = bf16[32,128,768]{2,1,0:T(8,128)(2,1)} async-done(((bf16[4,128,768]{2,1,0:T(8,128)(2,1)}), bf16[32,128,768]{2,1,0:T(8,128)(2,1)}) %all-gather.9.cloned.1.call-update) | async-done | bytes 6291472 | tf_op jit(solution)/shard_map/all_gather | solution.py:12
  89.1 3.8 %reduce_sum.71 = bf16[4,128,768]{2,1,0:T(8,128)(2,1)S(1)} reduce(bf16[8,4,128,768]{3,2,1,0:T(8,128)(2,1)} %bitcast.102, bf16[]{:T(256)} %constant.73.clone.1), dimensions={0}, to_apply=%region_2.3 | reduce | flops 2752512 | bytes 7077890 | tf_op jit(solution)/shard_map/reduce_sum | solution.py:13
  92.9 61.2 %all-gather.11.cloned.1.call-done = bf16[32,128,768]{2,1,0:T(8,128)(2,1)} async-done(((bf16[4,128,768]{2,1,0:T(8,128)(2,1)}), bf16[32,128,768]{2,1,0:T(8,128)(2,1)}) %all-gather.11.cloned.1.call-update) | async-done | bytes 6291472 | tf_op jit(solution)/shard_map/all_gather | solution.py:12
  154.1 4.8 %reduce_sum.72 = bf16[4,128,768]{2,1,0:T(8,128)(2,1)} reduce(bf16[8,4,128,768]{3,2,1,0:T(8,128)(2,1)} %bitcast.103, bf16[]{:T(256)} %constant.73.clone.1), dimensions={0}, to_apply=%region_3.4 | reduce | flops 2752512 | bytes 7077890 | tf_op jit(solution)/shard_map/reduce_sum | solution.py:13
  158.9 1.2 pad_maximum_fusion
  160.1 4.5 %convolution_convert_fusion = bf16[1024,1536]{1,0:T(8,128)(2,1)S(1)} fusion(bf16[1024,768]{1,0:T(8,128)(2,1)S(1)} %bitcast.104, bf16[768,2304]{1,0:T(8,128)(2,1)} %param.17), kind=kOutput, calls=%fused_computation.28 | convolution fusion | flops 2417491968 | bytes 7077888 | tf_op jit(solution)/shard_map/dot_general | solution.py:104
  164.6 1.9 fusion.48
  166.5 51.0 %while.30 = (s32[]{:T(128)}, f32[4,128,16]{1,2,0:T(8,128)}, f32[4,128,16]{1,2,0:T(8,128)}, f32[4,128,768]{2,1,0:T(8,128)}, bf16[4,128,768]{1,2,0:T(8,128)(2,1)},...) while((s32[]{:T(128)}, f32[4,128,16]{1,2,0:T(8,128)}, ...), condition=%wide.region_7.8_spmd.clone, body=%wide.region_4.7_spmd.clone.sunk | while | flops 106524672 | bytes 14295217 | solution.py:126
  168.8 3.2 select_reduce_fusion.2
  173.2 2.2 fusion.78
  176.3 2.3 fusion.77
  181.5 3.2 select_reduce_fusion.2
  185.9 2.2 fusion.78
  189.1 2.3 fusion.77
  194.3 3.2 select_reduce_fusion.2
  198.7 2.2 fusion.78
  201.8 2.3 fusion.77
  207.0 3.2 select_reduce_fusion.2
  211.4 2.2 fusion.78
  214.6 2.3 fusion.77
  218.2 8.4 %all-gather.2 = f32[16,128,16]{1,2,0:T(8,128)S(1)} all-gather(f32[4,128,16]{1,2,0:T(8,128)S(1)} %copy-done.3), channel_id=4, replica_groups=mesh['pb'=8,'ka'=4] {'ka'}, dimensions={0}, use_global_device_ids=true | all-gather | bytes 163840 | tf_op jit(solution)/shard_map/all_gather | solution.py:23
  226.7 10.6 %all-gather.3 = f32[16,128,16]{1,2,0:T(8,128)S(1)} all-gather(f32[4,128,16]{1,2,0:T(8,128)S(1)} %copy-done.4), channel_id=5, replica_groups=mesh['pb'=8,'ka'=4] {'ka'}, dimensions={0}, use_global_device_ids=true | all-gather | bytes 163840 | tf_op jit(solution)/shard_map/all_gather | solution.py:23
  237.2 50.0 %all-gather.13.cloned.1.call-done = f32[16,128,768]{2,1,0:T(8,128)} async-done(((f32[4,128,768]{2,1,0:T(8,128)}), f32[16,128,768]{2,1,0:T(8,128)}) %all-gather.13.cloned.1.call-update) | async-done | bytes 6291472 | tf_op jit(solution)/shard_map/all_gather | solution.py:23
  287.2 2.7 slice.60
  289.9 3.0 copy.29
  292.9 4.9 %slice.63 = f32[12,128,768]{2,1,0:T(8,128)} slice(f32[16,128,768]{2,1,0:T(8,128)} %all-gather.13.cloned.1.call-done), slice={[4:16], [0:128], [0:768]} | slice | bytes 9437184 | tf_op jit(solution)/shard_map/slice | solution.py:25
  297.8 26.9 %while.29 = (s32[]{:T(128)}, f32[4,128,16]{1,2,0:T(8,128)S(1)}, f32[4,128,16]{1,2,0:T(8,128)S(1)}, f32[4,128,768]{1,2,0:T(8,128)}, f32[3,4,128,16]{2,3,1,0:T(8,1...) while((s32[]{:T(128)}, f32[4,128,16]{1,2,0:T(8,128)S(1)}, ...), condition=%wide.region_9.10_spmd, body=%wide.region_8.9_spmd.sunk | while | flops 1228802 | bytes 11337821 | solution.py:26
  297.8 2.7 constant_dynamic-slice_fusion.9
  300.5 3.0 copy.46
  303.6 3.2 fusion.72
  306.8 2.7 constant_dynamic-slice_fusion.9
  309.5 3.0 copy.46
  312.5 3.2 fusion.72
  315.8 2.7 constant_dynamic-slice_fusion.9
  318.5 3.0 copy.46
  321.5 3.2 fusion.72
  324.7 3.0 copy.31
  328.3 1.2 div.37
  329.5 2.7 fusion.49
  332.6 3.1 fusion.54
  (134 shorter events, 27.2 us)
Async XLA Ops:
  6.5 329.2 %copy-start = (bf16[1536,768]{1,0:T(8,128)(2,1)S(1)}, bf16[1536,768]{1,0:T(8,128)(2,1)}, u32[]{:S(2)}) copy-start(bf16[1536,768]{1,0:T(8,128)(2,1)} %param.25) | copy-start | bytes 7077892
  6.5 82.6 %all-gather.9.cloned.1.call-start = ((), (), s32[]{:S(2)}) async-start(), calls=%async_computation | async-start | bytes 7077888 | tf_op jit(solution)/shard_map/all_gather | solution.py:12
  7.7 1.2 copy-start.5
  8.9 1.1 copy-start.11
  24.0 130.2 %all-gather.11.cloned.1.call-start = ((), (), s32[]{:S(2)}) async-start(), calls=%async_computation.1 | async-start | bytes 7077888 | tf_op jit(solution)/shard_map/all_gather | solution.py:12
  24.7 262.5 %all-gather.13.cloned.1.call-start = ((), (), s32[]{:S(2)}) async-start(), calls=%async_computation.2 | async-start | bytes 7864320 | tf_op jit(solution)/shard_map/all_gather | solution.py:23
  166.5 5.5 %copy-start.7 = (s32[128]{0:T(128)}, s32[128]{0:T(128)S(1)}, u32[]{:S(2)}) copy-start(s32[128]{0:T(128)S(1)} %get-tuple-element.398) | copy-start | bytes 1540 | tf_op jit(solution)/shard_map/while
  166.5 5.5 %copy-start.9 = (pred[128]{0:T(512)(128)(4,1)}, pred[128]{0:T(512)(128)(4,1)S(1)}, u32[]{:S(2)}) copy-start(pred[128]{0:T(512)(128)(4,1)S(1)} %get-tuple-element.396) | copy-start | bytes 388 | tf_op jit(solution)/shard_map/while
  168.7 3.2 copy-start.1
  175.3 1.0 copy-start.2
  175.5 3.7 %copy-start.8 = (s32[128]{0:T(128)S(1)}, s32[128]{0:T(128)}, u32[]{:S(2)}) copy-start(s32[128]{0:T(128)} %copy-done.7) | copy-start | bytes 1540 | tf_op jit(solution)/shard_map/while
  175.5 3.7 %copy-start.10 = (pred[128]{0:T(512)(128)(4,1)S(1)}, pred[128]{0:T(512)(128)(4,1)}, u32[]{:S(2)}) copy-start(pred[128]{0:T(512)(128)(4,1)} %copy-done.9) | copy-start | bytes 388 | tf_op jit(solution)/shard_map/while
  179.2 5.5 %copy-start.7 = (s32[128]{0:T(128)}, s32[128]{0:T(128)S(1)}, u32[]{:S(2)}) copy-start(s32[128]{0:T(128)S(1)} %get-tuple-element.398) | copy-start | bytes 1540 | tf_op jit(solution)/shard_map/while
  179.2 5.5 %copy-start.9 = (pred[128]{0:T(512)(128)(4,1)}, pred[128]{0:T(512)(128)(4,1)S(1)}, u32[]{:S(2)}) copy-start(pred[128]{0:T(512)(128)(4,1)S(1)} %get-tuple-element.396) | copy-start | bytes 388 | tf_op jit(solution)/shard_map/while
  181.5 3.2 copy-start.1
  188.1 1.0 copy-start.2
  188.3 3.7 %copy-start.8 = (s32[128]{0:T(128)S(1)}, s32[128]{0:T(128)}, u32[]{:S(2)}) copy-start(s32[128]{0:T(128)} %copy-done.7) | copy-start | bytes 1540 | tf_op jit(solution)/shard_map/while
  188.3 3.7 %copy-start.10 = (pred[128]{0:T(512)(128)(4,1)S(1)}, pred[128]{0:T(512)(128)(4,1)}, u32[]{:S(2)}) copy-start(pred[128]{0:T(512)(128)(4,1)} %copy-done.9) | copy-start | bytes 388 | tf_op jit(solution)/shard_map/while
  192.0 5.5 %copy-start.7 = (s32[128]{0:T(128)}, s32[128]{0:T(128)S(1)}, u32[]{:S(2)}) copy-start(s32[128]{0:T(128)S(1)} %get-tuple-element.398) | copy-start | bytes 1540 | tf_op jit(solution)/shard_map/while
  192.0 5.5 %copy-start.9 = (pred[128]{0:T(512)(128)(4,1)}, pred[128]{0:T(512)(128)(4,1)S(1)}, u32[]{:S(2)}) copy-start(pred[128]{0:T(512)(128)(4,1)S(1)} %get-tuple-element.396) | copy-start | bytes 388 | tf_op jit(solution)/shard_map/while
  194.3 3.2 copy-start.1
  200.8 1.0 copy-start.2
  201.0 3.7 %copy-start.8 = (s32[128]{0:T(128)S(1)}, s32[128]{0:T(128)}, u32[]{:S(2)}) copy-start(s32[128]{0:T(128)} %copy-done.7) | copy-start | bytes 1540 | tf_op jit(solution)/shard_map/while
  201.0 3.7 %copy-start.10 = (pred[128]{0:T(512)(128)(4,1)S(1)}, pred[128]{0:T(512)(128)(4,1)}, u32[]{:S(2)}) copy-start(pred[128]{0:T(512)(128)(4,1)} %copy-done.9) | copy-start | bytes 388 | tf_op jit(solution)/shard_map/while
  204.7 5.5 %copy-start.7 = (s32[128]{0:T(128)}, s32[128]{0:T(128)S(1)}, u32[]{:S(2)}) copy-start(s32[128]{0:T(128)S(1)} %get-tuple-element.398) | copy-start | bytes 1540 | tf_op jit(solution)/shard_map/while
  204.7 5.5 %copy-start.9 = (pred[128]{0:T(512)(128)(4,1)}, pred[128]{0:T(512)(128)(4,1)S(1)}, u32[]{:S(2)}) copy-start(pred[128]{0:T(512)(128)(4,1)S(1)} %get-tuple-element.396) | copy-start | bytes 388 | tf_op jit(solution)/shard_map/while
  207.0 3.2 copy-start.1
  213.6 1.0 copy-start.2
  213.8 3.7 %copy-start.8 = (s32[128]{0:T(128)S(1)}, s32[128]{0:T(128)}, u32[]{:S(2)}) copy-start(s32[128]{0:T(128)} %copy-done.7) | copy-start | bytes 1540 | tf_op jit(solution)/shard_map/while
  213.8 3.7 %copy-start.10 = (pred[128]{0:T(512)(128)(4,1)S(1)}, pred[128]{0:T(512)(128)(4,1)}, u32[]{:S(2)}) copy-start(pred[128]{0:T(512)(128)(4,1)} %copy-done.9) | copy-start | bytes 388 | tf_op jit(solution)/shard_map/while
  217.5 0.8 copy-start.3
  217.5 9.2 %copy-start.4 = (f32[4,128,16]{1,2,0:T(8,128)S(1)}, f32[4,128,16]{1,2,0:T(8,128)}, u32[]{:S(2)}) copy-start(f32[4,128,16]{1,2,0:T(8,128)} %get-tuple-element.93) | copy-start | bytes 98308
  327.8 1.7 copy-start.6
  327.8 1.7 copy-start.12
  327.8 1.7 copy-start.13
  329.5 3.0 copy-start.14
Sparse Core Ops, SparseCore 0:
  24.1 64.9 all-gather.8
  90.7 63.3 all-gather.10
  217.6 69.5 all-gather.12
